TPU v7x, 32 devices: a whole 2x2x4 slice. The times are simulated.
32 devices in a mesh: dp: 8 (over y, x, core), seq: 4 (over z).
Axes of the slice: x: 2, y: 2, z: 4, core: 2. Of those that a mesh axis runs over, the one named last changes fastest.
Arguments:
- hidden: bfloat16 [8192, 1792], P(('dp', 'seq')), may hold values from -12.75 to 12.75
- depths: int32 [8192], P(('dp', 'seq')), may hold values from 1 to 3, as said below
- packed_slot_index: int32 [8192], P(('dp', 'seq')), may hold values from -1 to 511, as said below
- value_weight: bfloat16 [1792, 1024], P('dp'), may hold values from -0.125 to 0.125
- output_weight: bfloat16 [1024, 1792], P('dp'), may hold values from -0.1875 to 0.1875
- adapter_down_factor: bfloat16 [1792, 128], P('dp'), may hold values from -0.125 to 0.125
- adapter_up_factor: bfloat16 [1024, 128], P('dp'), may hold values from -0.5 to 0.5
- before_norm_gain: float32 [1792], replicated, may hold values from 0.1 to 1.9
- after_norm_gain: float32 [1792], replicated, may hold values from 0.1 to 1.9
- cotangent: bfloat16 [4096, 1792], P(('dp', 'seq')), may hold values from -6 to 6
Outputs:
- looped: bfloat16 [4096, 1792], P(('dp', 'seq'))
- grad_hidden: bfloat16 [8192, 1792], P(('dp', 'seq'))
- down_factor_gradient: float32 [1792, 128], P('dp', 'seq')
- up_factor_gradient: float32 [1024, 128], P('dp', 'seq')
Inputs may be any that keep to these rules, and one draw needn't show every extreme that they name: `depths`: of the 1024 tokens of one dp index exactly 512 have depth 2 or 3, and all 256 tokens of one seq index are among them. -1 exactly where depths is 1. Over the tokens of one dp index with depth 2 or 3 the slots are a permutation of 0 to 511; packed_slot_index // 128 is the seq index that holds the token's packed row. At most 64 tokens of one device have slots of one seq index, and exactly 64 do in every dp index.
All inputs are finite; a program needn't handle non-finite values.
Results may differ from a plain program's by a relative error of at most 0.01.
Values may be sent and summed in bfloat16 or wider, within the bound.
A program may use at most 64 MiB of HBM per device.

v0:
```python
import math

import jax
import jax.numpy as jnp
from jax import lax
from jax.sharding import PartitionSpec as P

epsilon = 1e-06


def contract_final_axis(left, right):
    return lax.dot_general(
        left, right, (((1,), (1,)), ((), ())), preferred_element_type=jnp.float32
    )


def contract_first(left, right):
    return lax.dot_general(
        left, right, (((0,), (0,)), ((), ())), preferred_element_type=jnp.float32
    )


def layer_forward(
    input_rows,
    cotangent_rows,
    value_weight,
    output_weight,
    adapter_down_factor,
    adapter_up_factor,
    before_norm_gain,
    after_norm_gain,
):
    x_float = input_rows.astype(jnp.float32)
    inv_pre = lax.rsqrt(jnp.mean(x_float * x_float, axis=-1, keepdims=True) + epsilon)
    whitened = x_float * inv_pre
    normalized_rows = (whitened * before_norm_gain).astype(jnp.bfloat16)
    rank_reduced = jnp.dot(
        normalized_rows, adapter_down_factor, preferred_element_type=jnp.float32
    ).astype(jnp.bfloat16)
    projected_rows = (
        jnp.dot(normalized_rows, value_weight, preferred_element_type=jnp.float32)
        + contract_final_axis(rank_reduced, adapter_up_factor)
    ).astype(jnp.bfloat16)
    mixed_out = jnp.dot(projected_rows, output_weight, preferred_element_type=jnp.float32)
    inv_post = lax.rsqrt(jnp.mean(mixed_out * mixed_out, axis=-1, keepdims=True) + epsilon)
    shaped = mixed_out * inv_post
    looped = (x_float + shaped * after_norm_gain).astype(jnp.bfloat16)
    cot_float = cotangent_rows.astype(jnp.float32)
    grad_shaped = cot_float * after_norm_gain
    grad_mixed = (
        inv_post * (grad_shaped - shaped * jnp.mean(grad_shaped * shaped, axis=-1, keepdims=True))
    ).astype(jnp.bfloat16)
    value_gradient = contract_final_axis(grad_mixed, output_weight).astype(jnp.bfloat16)
    low_rank_gradient = jnp.dot(
        value_gradient, adapter_up_factor, preferred_element_type=jnp.float32
    ).astype(jnp.bfloat16)
    normalized_gradient = contract_final_axis(value_gradient, value_weight) + contract_final_axis(
        low_rank_gradient, adapter_down_factor
    )
    grad_white = normalized_gradient * before_norm_gain
    gradient_rows = (
        cot_float
        + inv_pre
        * (grad_white - whitened * jnp.mean(grad_white * whitened, axis=-1, keepdims=True))
    ).astype(jnp.bfloat16)
    down_factor_gradient = contract_first(normalized_rows, low_rank_gradient)
    up_factor_gradient = contract_first(value_gradient, rank_reduced)
    return (looped, gradient_rows, down_factor_gradient, up_factor_gradient)


def body(
    hidden,
    depths,
    packed_slot_index,
    value_weight,
    output_weight,
    adapter_down_factor,
    adapter_up_factor,
    before_norm_gain,
    after_norm_gain,
    cotangent,
):
    seq_count = lax.axis_size("seq")
    own_index = lax.axis_index("seq")
    tok_count = hidden.shape[0]
    act_rows = cotangent.shape[0]
    value_full, out_full, down_full, up_full = (
        lax.all_gather(value_weight, "dp", axis=0, tiled=True),
        lax.all_gather(output_weight, "dp", axis=0, tiled=True),
        lax.all_gather(adapter_down_factor, "dp", axis=0, tiled=True),
        lax.all_gather(adapter_up_factor, "dp", axis=0, tiled=True),
    )
    depth_all, slot_all = (
        lax.all_gather(depths, "seq", axis=0, tiled=True),
        lax.all_gather(packed_slot_index, "seq", axis=0, tiled=True),
    )
    active_all = depth_all >= 2
    dest_all = jnp.where(active_all, slot_all // act_rows, -1)
    pos_all = jnp.where(active_all, slot_all % act_rows, 0)
    mine = active_all & (dest_all == own_index)
    active = depths >= 2
    zero_row = jnp.zeros((), jnp.bfloat16)
    rows_all = lax.all_gather(hidden, "seq", axis=0, tiled=True)
    source = (
        jnp.zeros((act_rows,), jnp.int32)
        .at[jnp.where(mine, pos_all, act_rows)]
        .set(jnp.arange(seq_count * tok_count, dtype=jnp.int32), mode="drop")
    )
    packed = jnp.take(rows_all, source, axis=0)
    looped, gradient_rows, down_factor_gradient, up_factor_gradient = layer_forward(
        packed,
        cotangent,
        value_full,
        out_full,
        down_full,
        up_full,
        before_norm_gain,
        after_norm_gain,
    )
    grads_all = lax.all_gather(gradient_rows, "seq", axis=0, tiled=True)
    picked = jnp.take(grads_all, jnp.maximum(packed_slot_index, 0), axis=0)
    grad_hidden = jnp.where(active[:, None], picked, zero_row)
    grad_scale = 1.0 / math.sqrt(seq_count * act_rows * lax.axis_size("dp"))
    down_term = down_factor_gradient * grad_scale
    up_term = up_factor_gradient * grad_scale
    down_mid, up_mid = (
        lax.psum_scatter(
            down_term.astype(jnp.bfloat16), "seq", scatter_dimension=1, tiled=True
        ).astype(jnp.float32),
        lax.psum_scatter(
            up_term.astype(jnp.bfloat16), "seq", scatter_dimension=1, tiled=True
        ).astype(jnp.float32),
    )
    down_sum, up_sum = (
        lax.psum_scatter(down_mid, "dp", scatter_dimension=0, tiled=True),
        lax.psum_scatter(up_mid, "dp", scatter_dimension=0, tiled=True),
    )
    return (looped, grad_hidden, down_sum, up_sum)


def solution(mesh):
    placed = (
        P(("dp", "seq"), None),
        P(("dp", "seq")),
        P(("dp", "seq")),
        P("dp", None),
        P("dp", None),
        P("dp", None),
        P("dp", None),
        P(),
        P(),
        P(("dp", "seq"), None),
    )
    return jax.shard_map(
        body,
        mesh=mesh,
        in_specs=placed,
        out_specs=(P(("dp", "seq"), None), P(("dp", "seq"), None), P("dp", "seq"), P("dp", "seq")),
        check_vma=False,
    )
```

profile of v0, /device:TPU:0, one launch (start us, length us, event | category | flops | bytes accessed | tf_op | source)
XLA Modules:
  0.0 329.3 jit_solution(13722843027043391828)
XLA Ops:
  7.2 0.0 all-gather.7.cloned.1.call-start
  7.2 0.7 all-gather.7.cloned.1.call-update
  7.9 0.0 all-gather.9.cloned.1.call-start
  8.0 0.7 all-gather.9.cloned.1.call-update
  8.7 0.0 all-gather.11.cloned.1.call-start
  8.7 0.7 all-gather.11.cloned.1.call-update
  9.4 0.0 reduce-scatter.7.cloned.1.call-start
  9.4 12.8 %all-gather = s32[4,1,256]{2,1,0:T(1,128)S(1)} all-gather(s32[1,1,256]{2,1,0:T(1,128)} %bitcast.21), channel_id=1, replica_groups=mesh['dp'=8,'seq'=4] {'seq'}, dimensions={0}, use_global_device_ids=true | all-gather | bytes 5120 | tf_op jit(solution)/shard_map/all_gather | solution.py:94
  22.3 8.1 %all-gather.1 = s32[4,1,256]{2,1,0:T(1,128)S(1)} all-gather(s32[1,1,256]{2,1,0:T(1,128)} %bitcast.20), channel_id=1, replica_groups=mesh['dp'=8,'seq'=4] {'seq'}, dimensions={0}, use_global_device_ids=true | all-gather | bytes 5120 | tf_op jit(solution)/shard_map/all_gather | solution.py:95
  30.4 4.3 %scatter_custom_fusion = s32[128]{0:T(128)S(1)} fusion(s32[1024]{0:T(1024)S(1)} %compare_select_fusion, s32[1024]{0:T(1024)S(1)} %iota.3, s32[]{:T(128)} %constant.69.clone.1), kind=kCustom, calls=%fused_computation.69 | custom fusion | bytes 516 | tf_op jit(solution)/shard_map/scatter | solution.py:107
  34.8 9.5 %all_gather.29 = bf16[1024,128]{1,0:T(8,128)(2,1)S(1)} all-gather(bf16[128,128]{1,0:T(8,128)(2,1)} %param.16), channel_id=1, replica_groups=mesh['dp'=8,'seq'=4] {'dp'}, dimensions={0}, use_global_device_ids=true | all-gather | bytes 294912 | tf_op jit(solution)/shard_map/all_gather | solution.py:91
  44.3 9.5 %all_gather.28 = bf16[1792,128]{1,0:T(8,128)(2,1)S(1)} all-gather(bf16[224,128]{1,0:T(8,128)(2,1)} %param.15), channel_id=1, replica_groups=mesh['dp'=8,'seq'=4] {'dp'}, dimensions={0}, use_global_device_ids=true | all-gather | bytes 516096 | tf_op jit(solution)/shard_map/all_gather | solution.py:90
  53.8 30.7 %all-gather.7.cloned.1.call-done = bf16[1024,1792]{1,0:T(8,128)(2,1)} async-done(((bf16[256,1792]{1,0:T(8,128)(2,1)}), bf16[1024,1792]{1,0:T(8,128)(2,1)}) %all-gather.7.cloned.1.call-update) | async-done | bytes 3670032 | tf_op jit(solution)/shard_map/all_gather | solution.py:103
  84.5 3.8 %gather_fusion = bf16[128,1792]{1,0:T(8,128)(2,1)S(1)} fusion(bf16[1024,1792]{1,0:T(8,128)(2,1)} %all-gather.7.cloned.1.call-done, s32[1024]{0:T(1024)S(1)} %pad_clamp_fusion.1), kind=kCustom, calls=%fused_computation | custom fusion | bytes 918016 | tf_op jit(solution)/shard_map/jit(_take)/gather | solution.py:109
  88.4 0.3 fusion.18
  88.7 0.4 convolution_convert_fusion.1
  89.0 30.5 %all-gather.9.cloned.1.call-done = bf16[1792,1024]{1,0:T(8,128)(2,1)} async-done(((bf16[224,1024]{1,0:T(8,128)(2,1)}), bf16[1792,1024]{1,0:T(8,128)(2,1)}) %all-gather.9.cloned.1.call-update) | async-done | bytes 3670032 | tf_op jit(solution)/shard_map/all_gather | solution.py:88
  119.5 2.7 fusion.37
  122.3 0.0 copy-start
  122.3 33.7 %all-gather.11.cloned.1.call-done = bf16[1024,1792]{1,0:T(8,128)(2,1)} async-done(((bf16[128,1792]{1,0:T(8,128)(2,1)}), bf16[1024,1792]{1,0:T(8,128)(2,1)}) %all-gather.11.cloned.1.call-update) | async-done | bytes 3670032 | tf_op jit(solution)/shard_map/all_gather | solution.py:89
  156.0 2.9 multiply_reduce_fusion
  158.9 1.1 fusion.10
  160.0 3.4 %convolution_convert_fusion = bf16[128,1024]{1,0:T(8,128)(2,1)S(1)} fusion(bf16[1024,1792]{1,0:T(8,128)(2,1)} %all-gather.11.cloned.1.call-done, bf16[128,1792]{1,0:T(8,128)(2,1)S(1)} %copy-done, f32[128,1792]{1,0:T(8,128)S(1)} %get-tuple-element.7, f32[128]{0:T(128)S(1)} %broadcast_multiply_fusion.1, f32[1792]{0:T(1024)S(1)} %copy-done.1, ...), kind=kOutput, calls=%fused_computation.15 | convolution fusion | flops 471498752 | bytes 5316608 | tf_op jit(solution)/shard_map/dot_general | solution.py:12
  163.4 0.2 convolution_convert_fusion.2
  163.6 1.2 fusion.1
  164.8 0.0 reduce-scatter.7.cloned.1.call-update
  164.8 0.0 reduce-scatter.9.cloned.1.call-start
  164.9 1.0 fusion.6
  165.8 0.0 reduce-scatter.9.cloned.1.call-update
  165.8 0.0 reduce-scatter.13.cloned.1.call-start
  165.9 3.4 %fusion.39 = f32[128,1792]{1,0:T(8,128)S(1)} fusion(bf16[128,1024]{1,0:T(8,128)(2,1)S(1)} %convolution_convert_fusion, bf16[1792,1024]{1,0:T(8,128)(2,1)} %all-gather.9.cloned.1.call-done), kind=kOutput, calls=%fused_computation.72 | convolution fusion | flops 469762048 | bytes 4849664 | tf_op jit(solution)/shard_map/dot_general | solution.py:12
  169.3 0.4 fusion.15
  169.8 16.2 %reduce-scatter.7.cloned.1.call-done = bf16[1792,32]{0,1:T(8,128)(2,1)} async-done(((bf16[1792,128]{0,1:T(8,128)(2,1)}), bf16[1792,32]{0,1:T(8,128)(2,1)}) %reduce-scatter.7.cloned.1.call-update) | async-done | bytes 114704 | tf_op jit(solution)/shard_map/reduce_scatter | solution.py:127
  186.0 2.0 copy.14
  188.0 0.0 reduce-scatter.13.cloned.1.call-update
  188.0 0.0 all-gather.13.cloned.1.call-start
  188.1 1.3 fusion.13
  189.4 0.0 all-gather.13.cloned.1.call-update
  189.4 0.0 reduce-scatter.11.cloned.1.call-start
  189.6 16.7 %reduce-scatter.9.cloned.1.call-done = bf16[1024,32]{0,1:T(8,128)(2,1)} async-done(((bf16[1024,128]{0,1:T(8,128)(2,1)}), bf16[1024,32]{0,1:T(8,128)(2,1)}) %reduce-scatter.9.cloned.1.call-update) | async-done | bytes 65552 | tf_op jit(solution)/shard_map/reduce_scatter | solution.py:130
  206.3 1.5 convert_element_type.55
  207.8 0.0 reduce-scatter.11.cloned.1.call-update
  207.8 35.8 %reduce-scatter.13.cloned.1.call-done = f32[224,32]{1,0:T(8,128)} async-done(((f32[1792,32]{1,0:T(8,128)}), f32[224,32]{1,0:T(8,128)}) %reduce-scatter.13.cloned.1.call-update) | async-done | bytes 28688
  243.6 1.6 copy.15
  245.2 41.4 %all-gather.13.cloned.1.call-done = bf16[512,1792]{1,0:T(8,128)(2,1)} async-done(((bf16[128,1792]{1,0:T(8,128)(2,1)}), bf16[512,1792]{1,0:T(8,128)(2,1)}) %all-gather.13.cloned.1.call-update) | async-done | bytes 1835024 | tf_op jit(solution)/shard_map/all_gather | solution.py:120
  286.6 3.9 %gather_fusion.1 = bf16[256,1792]{1,0:T(8,128)(2,1)S(1)} fusion(bf16[512,1792]{1,0:T(8,128)(2,1)} %all-gather.13.cloned.1.call-done, s32[1024]{0:T(1024)S(1)} %pad_clamp_fusion), kind=kCustom, calls=%fused_computation.1 | custom fusion | bytes 1836032 | tf_op jit(solution)/shard_map/jit(_take)/gather | solution.py:121
  290.5 1.1 select_select_fusion
  291.6 30.8 %reduce-scatter.11.cloned.1.call-done = f32[128,32]{0,1:T(8,128)} async-done(((f32[1024,32]{0,1:T(8,128)}), f32[128,32]{0,1:T(8,128)}) %reduce-scatter.11.cloned.1.call-update) | async-done | bytes 16400 | tf_op jit(solution)/shard_map/reduce_scatter | solution.py:136
  (24 shorter events, 0.1 us)
Async XLA Ops:
  7.2 81.5 %copy-start.2 = (f32[1792]{0:T(1024)S(1)}, f32[1792]{0:T(1024)}, u32[]{:S(2)}) copy-start(f32[1792]{0:T(1024)} %param.17) | copy-start | bytes 21508
  7.2 77.3 %all-gather.7.cloned.1.call-start = ((), (), s32[]{:S(2)}) async-start(), calls=%async_computation.4 | async-start | bytes 4587520 | tf_op jit(solution)/shard_map/all_gather | solution.py:103
  7.9 111.6 %all-gather.9.cloned.1.call-start = ((), (), s32[]{:S(2)}) async-start(), calls=%async_computation.5 | async-start | bytes 4128768 | tf_op jit(solution)/shard_map/all_gather | solution.py:88
  8.7 147.3 %all-gather.11.cloned.1.call-start = ((), (), s32[]{:S(2)}) async-start(), calls=%async_computation.6 | async-start | bytes 4128768 | tf_op jit(solution)/shard_map/all_gather | solution.py:89
  9.4 176.6 %reduce-scatter.7.cloned.1.call-start = ((), (), s32[]{:S(2)}) async-start(), calls=%async_computation.8 | async-start | bytes 573440 | tf_op jit(solution)/shard_map/reduce_scatter | solution.py:127
  122.3 36.7 %copy-start = (bf16[128,1792]{1,0:T(8,128)(2,1)S(1)}, bf16[128,1792]{1,0:T(8,128)(2,1)}, u32[]{:S(2)}) copy-start(bf16[128,1792]{1,0:T(8,128)(2,1)} %param.19) | copy-start | bytes 1376260
  122.3 36.6 %copy-start.1 = (f32[1792]{0:T(1024)S(1)}, f32[1792]{0:T(1024)}, u32[]{:S(2)}) copy-start(f32[1792]{0:T(1024)} %param.18) | copy-start | bytes 21508
  164.8 41.5 %reduce-scatter.9.cloned.1.call-start = ((), (), s32[]{:S(2)}) async-start(), calls=%async_computation.9 | async-start | bytes 327680 | tf_op jit(solution)/shard_map/reduce_scatter | solution.py:130
  165.8 77.8 %reduce-scatter.13.cloned.1.call-start = ((), (), s32[]{:S(2)}) async-start(), calls=%async_computation.11 | async-start | bytes 1032192
  169.3 20.2 %copy-start.3 = (s32[256]{0:T(256)S(1)}, s32[256]{0:T(256)}, u32[]{:S(2)}) copy-start(s32[256]{0:T(256)} %param.12) | copy-start | bytes 3076
  169.3 20.3 %copy-start.4 = (s32[256]{0:T(256)S(1)}, s32[256]{0:T(256)}, u32[]{:S(2)}) copy-start(s32[256]{0:T(256)} %param.11) | copy-start | bytes 3076
  188.0 98.6 %all-gather.13.cloned.1.call-start = ((), (), s32[]{:S(2)}) async-start(), calls=%async_computation.7 | async-start | bytes 2293760 | tf_op jit(solution)/shard_map/all_gather | solution.py:120
  189.4 133.0 %reduce-scatter.11.cloned.1.call-start = ((), (), s32[]{:S(2)}) async-start(), calls=%async_computation.10 | async-start | bytes 147456 | tf_op jit(solution)/shard_map/reduce_scatter | solution.py:136
Sparse Core Ops, SparseCore 0:
  9.6 74.8 all-gather.6
  86.4 33.0 all-gather.8
  121.4 34.5 all-gather.10
  164.9 20.9 reduce-scatter.6
  188.2 18.0 reduce-scatter.8
  209.9 33.6 reduce-scatter.12
  245.2 41.3 all-gather.12
  290.2 32.2 reduce-scatter.10
where the time goes:
time: 330 us; the launch traced here: 329 us
  waiting for transfers between devices  238 us (72%)
  blocking collectives  39.9 us (12%)
  local copies, waits for them, and re-layouts  15.7 us (5%)
  matrix products  15.5 us (5%)
  between operations  14.3 us (4%)
  other arithmetic  5.43 us (2%)
    all_gather x1, waiting for transfers between devices, body(): grads_all = lax.all_gather(gradient_rows, 'seq', axis=0, tiled=True)  41.4 us
    unnamed x9, waiting for transfers between devices  38 us
    all_gather x1, waiting for transfers between devices, body(): lax.all_gather(output_weight, 'dp', axis=0, tiled=True)  33.7 us
    reduce_scatter x1, waiting for transfers between devices, body(): lax.psum_scatter(up_mid, 'dp', scatter_dimension=0, tiled=True)  30.8 us
    all_gather x1, waiting for transfers between devices, body(): rows_all = lax.all_gather(hidden, 'seq', axis=0, tiled=True)  30.7 us
    all_gather x1, waiting for transfers between devices, body(): lax.all_gather(value_weight, 'dp', axis=0, tiled=True)  30.5 us
    reduce_scatter x1, waiting for transfers between devices, body(): lax.psum_scatter(up_term.astype(jnp.bfloat16), 'seq', scatter_dimension=1...  16.7 us
    reduce_scatter x1, waiting for transfers between devices, body(): lax.psum_scatter(down_term.astype(jnp.bfloat16), 'seq', scatter_dimension...  16.2 us
  transfers between devices with their start and end apart: 8, of which 8 were waited for; matrix products, arithmetic and copies ran while one was open for 8% of the time, Pallas kernels for 0%

commit v1 on v0

--- a/solution.py
+++ b/solution.py
@@ -1,8 +1,11 @@
+import functools
 import math
 
 import jax
 import jax.numpy as jnp
 from jax import lax
+from jax.experimental import pallas as pl
+from jax.experimental.pallas import tpu as pltpu
 from jax.sharding import PartitionSpec as P
 
 epsilon = 1e-06
@@ -68,7 +71,7 @@
     return (looped, gradient_rows, down_factor_gradient, up_factor_gradient)
 
 
-def body(
+def general_body(
     hidden,
     depths,
     packed_slot_index,
@@ -138,6 +141,404 @@
     return (looped, grad_hidden, down_sum, up_sum)
 
 
+MESH = pl.DeviceIdType.MESH
+BF, F32 = jnp.bfloat16, jnp.float32
+CAP = 64
+
+
+def dot(left, right, left_axis=1, right_axis=0):
+    return lax.dot_general(
+        left, right, (((left_axis,), (right_axis,)), ((), ())), preferred_element_type=F32
+    )
+
+
+def fused_kernel(
+    slot_ref, depth_ref, gain_b_ref, gain_a_ref, hidden_hbm, cot_hbm, wv_in, wo_in, dn_in, up_in,
+    looped_hbm, gh_hbm, down_out, up_out,
+    wv, wo, dn, up, hid, cot, sendb, recvb, gsend, grecv, lsend, lrecv, zsend, zrecv,
+    place, unplace, normed, low, proj, mixed, gv, gn, packed, looped,
+    w_send, w_recv, s_send, s_recv, l_send, l_recv, g_send, g_recv, z_send, z_recv, loc,
+):
+    dp, seq = lax.axis_index("dp"), lax.axis_index("seq")
+    n_dp, n_seq = 8, 4
+    width = hid.shape[1]
+    core, x, y = dp % 2, (dp // 2) % 2, dp // 4
+    nbr_x, nbr_y, sib = dp + 2 - 4 * x, dp + 4 - 8 * y, dp + 1 - 2 * core
+    diag = nbr_x + 4 - 8 * y
+    to_sib = 1 - 2 * core
+
+    local = [
+        pltpu.make_async_copy(hidden_hbm, hid, loc.at[0]),
+        pltpu.make_async_copy(cot_hbm, cot, loc.at[1]),
+    ]
+    arrays = [(dn_in, dn), (up_in, up), (wv_in, wv), (wo_in, wo)]
+    for number, (shard, full) in enumerate(arrays):
+        rows = shard.shape[0]
+        local.append(
+            pltpu.make_async_copy(
+                shard, full.at[pl.ds(pl.multiple_of(dp * rows, 16), rows), :], loc.at[2 + number]
+            )
+        )
+    for copy in local:
+        copy.start()
+
+    barrier = pltpu.get_barrier_semaphore()
+    for k in range(1, n_dp):
+        pl.semaphore_signal(barrier, inc=1, device_id=((dp + k) % n_dp, seq), device_id_type=MESH)
+    for k in range(1, n_seq):
+        pl.semaphore_signal(barrier, inc=1, device_id=(dp, (seq + k) % n_seq), device_id_type=MESH)
+
+    tok = hid.shape[0]
+    slots = slot_ref[...]
+    act = depth_ref[...] >= 2
+    dest = jnp.where(act, slots // 128, -1)
+    where_to = lax.broadcasted_iota(jnp.int32, (8, tok), 0) == dest
+    earlier = (
+        lax.broadcasted_iota(jnp.int32, (tok, tok), 0)
+        < lax.broadcasted_iota(jnp.int32, (tok, tok), 1)
+    ).astype(F32).astype(BF)
+    counts = dot(where_to.astype(F32).astype(BF), earlier)
+    rank = jnp.sum(jnp.where(where_to, counts, 0.0), axis=0, keepdims=True)
+    row_of = jnp.where(act, dest.astype(F32) * CAP + rank, -1.0)
+    picked = (lax.broadcasted_iota(jnp.int32, (n_seq * CAP, tok), 0).astype(F32) == row_of).astype(F32)
+    place[...] = picked.astype(BF)
+    position = jnp.where(act, slots - dest * 128 + 1, 0).astype(F32)
+    pos_col = jnp.sum(picked * position, axis=1, keepdims=True) - 1.0
+    sendb[:, width:] = jnp.broadcast_to(pos_col, (n_seq * CAP, 128)).astype(BF)
+
+    pl.semaphore_wait(barrier, n_dp - 1 + n_seq - 1)
+
+    def region(a, owner, half):
+        shard, full = arrays[a]
+        rows = shard.shape[0]
+        if half is None:
+            return full.at[pl.ds(pl.multiple_of(owner * rows, 16), rows), :]
+        part = rows // 2
+        return full.at[pl.ds(pl.multiple_of(owner * rows + half * part, 16), part), :]
+
+    def piece(a, number, owner, half, target, from_input=False):
+        dst = region(a, owner, half)
+        if from_input:
+            shard = arrays[a][0]
+            part = shard.shape[0] // 2
+            source = shard if half is None else shard.at[pl.ds(half * part, part), :]
+        else:
+            source = dst
+        return pltpu.make_async_remote_copy(
+            src_ref=source, dst_ref=dst, send_sem=w_send.at[a * 13 + number],
+            recv_sem=w_recv.at[a * 13 + number], device_id=(target, seq), device_id_type=MESH,
+        )
+
+    pending = []
+
+    def send(*args, **kw):
+        copy = piece(*args, **kw)
+        copy.start()
+        pending.append(copy)
+
+    def got(a, number, owner, half):
+        piece(a, number, owner, half, sib).wait_recv()
+
+    def own(a):
+        send(a, 0, dp, 0, nbr_x, from_input=True)
+        send(a, 3, dp, 1, nbr_y, from_input=True)
+        send(a, 1, dp, 1, nbr_x, from_input=True)
+        send(a, 2, dp, 0, nbr_y, from_input=True)
+        send(a, 6, dp, None, sib, from_input=True)
+
+    def forward_first(a):
+        got(a, 0, nbr_x, 0)
+        send(a, 4, nbr_x, 0, nbr_y)
+        send(a, 7, nbr_x, 0, sib)
+        got(a, 3, nbr_y, 1)
+        send(a, 5, nbr_y, 1, nbr_x)
+        send(a, 8, nbr_y, 1, sib)
+
+    def forward_second(a):
+        got(a, 1, nbr_x, 1)
+        send(a, 9, nbr_x, 1, sib)
+        got(a, 2, nbr_y, 0)
+        send(a, 10, nbr_y, 0, sib)
+
+    def forward_diag(a):
+        got(a, 4, diag, 0)
+        send(a, 11, diag, 0, sib)
+        got(a, 5, diag, 1)
+        send(a, 12, diag, 1, sib)
+
+    def finish(a):
+        got(a, 6, sib, None)
+        got(a, 7, nbr_x + to_sib, 0)
+        got(a, 8, nbr_y + to_sib, 1)
+        got(a, 9, nbr_x + to_sib, 1)
+        got(a, 10, nbr_y + to_sib, 0)
+        got(a, 11, diag + to_sib, 0)
+        got(a, 12, diag + to_sib, 1)
+
+    for a in (0, 1, 2):
+        own(a)
+
+    def block(owner, rows):
+        return pl.ds(pl.multiple_of(owner * rows, 16), rows)
+
+    def exchange(src_buf, dst_buf, sends, recvs, k):
+        target = (seq + k) % n_seq
+        return pltpu.make_async_remote_copy(
+            src_ref=src_buf.at[block(target, CAP), :], dst_ref=dst_buf.at[block(seq, CAP), :],
+            send_sem=sends.at[k], recv_sem=recvs.at[k], device_id=(dp, target), device_id_type=MESH,
+        )
+
+    def arrival(src_buf, dst_buf, sends, recvs, k):
+        origin = (seq + n_seq - k) % n_seq
+        here = dst_buf.at[block(origin, CAP), :]
+        pltpu.make_async_remote_copy(
+            src_ref=here, dst_ref=here, send_sem=sends.at[k], recv_sem=recvs.at[k],
+            device_id=(dp, origin), device_id_type=MESH,
+        ).wait_recv()
+
+    local[0].wait()
+    sendb[:, :width] = dot(place[...], hid[...]).astype(BF)
+    for k in (2, 1, 3):
+        copy = exchange(sendb, recvb, s_send, s_recv, k)
+        copy.start()
+        pending.append(copy)
+    recvb[block(seq, CAP), :] = sendb[block(seq, CAP), :]
+
+    for a in (0, 1, 2):
+        forward_first(a)
+    own(3)
+    for a in (0, 1, 2):
+        forward_second(a)
+
+    for k in (1, 2, 3):
+        arrival(sendb, recvb, s_send, s_recv, k)
+    lanes = lax.broadcasted_iota(jnp.int32, (n_seq * CAP, 128), 1).astype(F32)
+    unplace[...] = (recvb[:, width:].astype(F32) == lanes).astype(F32).astype(BF)
+    x_float = dot(unplace[...], recvb[:, :width], 0, 0)
+    packed[...] = x_float
+    inv_pre = lax.rsqrt(jnp.mean(x_float * x_float, axis=-1, keepdims=True) + epsilon)
+    normed[...] = (x_float * inv_pre * gain_b_ref[...]).astype(BF)
+
+    for a in (0, 1, 2):
+        forward_diag(a)
+    for copy in local[1:]:
+        copy.wait()
+    for a in (0, 1, 2):
+        finish(a)
+
+    low[...] = dot(normed[...], dn[...]).astype(BF)
+
+    tile = 256
+
+    @pl.loop(0, proj.shape[1] // tile)
+    def _(n):
+        at = pl.ds(pl.multiple_of(n * tile, tile), tile)
+        proj[:, at] = (
+            dot(normed[...], wv[:, at]) + dot(low[...], up[at, :], 1, 1)
+        ).astype(BF)
+
+    forward_first(3)
+    forward_second(3)
+    forward_diag(3)
+    finish(3)
+
+    @pl.loop(0, width // tile)
+    def _(n):
+        at = pl.ds(pl.multiple_of(n * tile, tile), tile)
+        mixed[:, at] = dot(proj[...], wo[:, at])
+
+    m = mixed[...]
+    inv_post = lax.rsqrt(jnp.mean(m * m, axis=-1, keepdims=True) + epsilon)
+    shaped = m * inv_post
+    gain_a = gain_a_ref[...]
+    looped[...] = (packed[...] + shaped * gain_a).astype(BF)
+    loop_out = pltpu.make_async_copy(looped, looped_hbm, loc.at[6])
+    loop_out.start()
+    grad_shaped = cot[...].astype(F32) * gain_a
+    mixed[...] = inv_post * (
+        grad_shaped - shaped * jnp.mean(grad_shaped * shaped, axis=-1, keepdims=True)
+    )
+
+    @pl.loop(0, gv.shape[1] // tile)
+    def _(n):
+        at = pl.ds(pl.multiple_of(n * tile, tile), tile)
+        gv[:, at] = dot(mixed[...].astype(BF), wo[at, :], 1, 1).astype(BF)
+
+    grad_low = dot(gv[...], up[...]).astype(BF)
+
+    down_rows, up_rows = down_out.shape[0], up_out.shape[0]
+    down_term = dot(normed[...], grad_low, 0, 0).astype(BF)
+    up_term = dot(gv[...], low[...], 0, 0).astype(BF)
+    for owner in range(n_dp):
+        lsend[owner, :down_rows, :] = down_term[owner * down_rows : (owner + 1) * down_rows, :]
+        lsend[owner, down_rows:, :] = up_term[owner * up_rows : (owner + 1) * up_rows, :]
+    for k in range(1, n_dp):
+        target = (dp + k) % n_dp
+        copy = pltpu.make_async_remote_copy(
+            src_ref=lsend.at[target], dst_ref=lrecv.at[dp], send_sem=l_send.at[k],
+            recv_sem=l_recv.at[k], device_id=(target, seq), device_id_type=MESH,
+        )
+        copy.start()
+        pending.append(copy)
+    lrecv[dp] = lsend[dp]
+
+    @pl.loop(0, width // tile)
+    def _(n):
+        at = pl.ds(pl.multiple_of(n * tile, tile), tile)
+        gn[:, at] = dot(gv[...], wv[at, :], 1, 1) + dot(grad_low, dn[at, :], 1, 1)
+
+    x_float = packed[...]
+    inv_pre = lax.rsqrt(jnp.mean(x_float * x_float, axis=-1, keepdims=True) + epsilon)
+    whitened = x_float * inv_pre
+    grad_white = gn[...] * gain_b_ref[...]
+    grad_packed = (
+        cot[...].astype(F32)
+        + inv_pre
+        * (grad_white - whitened * jnp.mean(grad_white * whitened, axis=-1, keepdims=True))
+    ).astype(BF)
+    gsend[...] = dot(unplace[...], grad_packed).astype(BF)
+    for k in (2, 1, 3):
+        copy = exchange(gsend, grecv, g_send, g_recv, k)
+        copy.start()
+        pending.append(copy)
+    grecv[block(seq, CAP), :] = gsend[block(seq, CAP), :]
+
+    for k in range(1, n_dp):
+        origin = (dp + n_dp - k) % n_dp
+        here = lrecv.at[origin]
+        pltpu.make_async_remote_copy(
+            src_ref=here, dst_ref=here, send_sem=l_send.at[k], recv_sem=l_recv.at[k],
+            device_id=(origin, seq), device_id_type=MESH,
+        ).wait_recv()
+    total = lrecv[0].astype(F32)
+    for owner in range(1, n_dp):
+        total += lrecv[owner].astype(F32)
+    lead = total.shape[0]
+    pad = zsend.shape[1] - lead
+    total = jnp.concatenate([total, jnp.zeros((pad, total.shape[1]), F32)], axis=0)
+    zsend[...] = total.T
+    cols = down_out.shape[1]
+    for k in range(1, n_seq):
+        target = (seq + k) % n_seq
+        copy = pltpu.make_async_remote_copy(
+            src_ref=zsend.at[pl.ds(pl.multiple_of(target * cols, 8), cols), :],
+            dst_ref=zrecv.at[seq], send_sem=z_send.at[k], recv_sem=z_recv.at[k],
+            device_id=(dp, target), device_id_type=MESH,
+        )
+        copy.start()
+        pending.append(copy)
+    zrecv[seq] = zsend[pl.ds(pl.multiple_of(seq * cols, 8), cols), :]
+
+    for k in (1, 2, 3):
+        arrival(gsend, grecv, g_send, g_recv, k)
+    hid[...] = dot(place[...], grecv[...], 0, 0).astype(BF)
+    grad_out = pltpu.make_async_copy(hid, gh_hbm, loc.at[7])
+    grad_out.start()
+
+    for k in range(1, n_seq):
+        origin = (seq + n_seq - k) % n_seq
+        here = zrecv.at[origin]
+        pltpu.make_async_remote_copy(
+            src_ref=here, dst_ref=here, send_sem=z_send.at[k], recv_sem=z_recv.at[k],
+            device_id=(dp, origin), device_id_type=MESH,
+        ).wait_recv()
+    grad_scale = 1.0 / math.sqrt(n_seq * cot.shape[0] * n_dp)
+    mine = ((zrecv[0] + zrecv[1]) + (zrecv[2] + zrecv[3])) * grad_scale
+    mine = jnp.concatenate([mine, jnp.zeros((128 - cols, mine.shape[1]), F32)], axis=0).T
+    down_out[...] = mine[:down_rows, :cols]
+    up_out[...] = mine[down_rows:lead, :cols]
+    for copy in pending:
+        copy.wait_send()
+    loop_out.wait()
+    grad_out.wait()
+
+
+def fused_body(
+    hidden, depths, packed_slot_index, value_weight, output_weight, adapter_down_factor,
+    adapter_up_factor, before_norm_gain, after_norm_gain, cotangent,
+):
+    tok, width = hidden.shape
+    act = cotangent.shape[0]
+    n_dp, n_seq = lax.axis_size("dp"), lax.axis_size("seq")
+    v_rows, value_width = value_weight.shape
+    o_rows = output_weight.shape[0]
+    rank = adapter_up_factor.shape[1]
+    u_rows = adapter_up_factor.shape[0]
+    cols = rank // n_seq
+    lead = v_rows + u_rows
+    lead_pad = -(-lead // 128) * 128
+    vm, hbm = pl.BlockSpec(memory_space=pltpu.VMEM), pl.BlockSpec(memory_space=pl.ANY)
+    dma = pltpu.SemaphoreType.DMA
+    rows = n_seq * CAP
+    return pl.pallas_call(
+        fused_kernel,
+        out_shape=(
+            jax.ShapeDtypeStruct((act, width), BF),
+            jax.ShapeDtypeStruct((tok, width), BF),
+            jax.ShapeDtypeStruct((v_rows, cols), F32),
+            jax.ShapeDtypeStruct((u_rows, cols), F32),
+        ),
+        in_specs=[vm] * 4 + [hbm] * 6,
+        out_specs=(hbm, hbm, vm, vm),
+        scratch_shapes=[
+            pltpu.VMEM((v_rows * n_dp, value_width), BF),
+            pltpu.VMEM((o_rows * n_dp, width), BF),
+            pltpu.VMEM((v_rows * n_dp, rank), BF),
+            pltpu.VMEM((u_rows * n_dp, rank), BF),
+            pltpu.VMEM((tok, width), BF),
+            pltpu.VMEM((act, width), BF),
+            pltpu.VMEM((rows, width + 128), BF),
+            pltpu.VMEM((rows, width + 128), BF),
+            pltpu.VMEM((rows, width), BF),
+            pltpu.VMEM((rows, width), BF),
+            pltpu.VMEM((n_dp, lead, rank), BF),
+            pltpu.VMEM((n_dp, lead, rank), BF),
+            pltpu.VMEM((rank, lead_pad), F32),
+            pltpu.VMEM((n_seq, cols, lead_pad), F32),
+            pltpu.VMEM((rows, tok), BF),
+            pltpu.VMEM((rows, 128), BF),
+            pltpu.VMEM((act, width), BF),
+            pltpu.VMEM((act, rank), BF),
+            pltpu.VMEM((act, value_width), BF),
+            pltpu.VMEM((act, width), F32),
+            pltpu.VMEM((act, value_width), BF),
+            pltpu.VMEM((act, width), F32),
+            pltpu.VMEM((act, width), F32),
+            pltpu.VMEM((act, width), BF),
+            dma((52,)), dma((52,)), dma((4,)), dma((4,)), dma((8,)), dma((8,)),
+            dma((4,)), dma((4,)), dma((4,)), dma((4,)), dma((8,)),
+        ],
+        compiler_params=pltpu.CompilerParams(
+            collective_id=0, has_side_effects=True, vmem_limit_bytes=48 << 20
+        ),
+    )(
+        packed_slot_index.reshape(1, tok),
+        depths.reshape(1, tok),
+        before_norm_gain.reshape(1, width),
+        after_norm_gain.reshape(1, width),
+        hidden,
+        cotangent,
+        value_weight,
+        output_weight,
+        adapter_down_factor,
+        adapter_up_factor,
+    )
+
+
+def body(*arrays):
+    fits = (
+        lax.axis_size("dp") == 8
+        and lax.axis_size("seq") == 4
+        and arrays[0].shape[0] == 4 * CAP
+        and arrays[9].shape[0] == 128
+        and arrays[0].shape[1] % 256 == 0
+        and arrays[3].shape[1] % 256 == 0
+        and all(arrays[i].shape[0] % 32 == 0 for i in (3, 4, 5, 6))
+        and arrays[6].shape[1] == 128
+    )
+    return (fused_body if fits else general_body)(*arrays)
+
+
 def solution(mesh):
     placed = (
         P(("dp", "seq"), None),

time: 330 us -> 88.3 us (0.27)
  waiting for transfers between devices: 238 us -> 0 us
  Pallas kernels: 0 us -> 76.9 us
  blocking collectives: 39.9 us -> 0 us
  matrix products: 15.5 us -> 0 us
  between operations: 14.3 us -> 0.67 us
  local copies, waits for them, and re-layouts: 15.7 us -> 10.2 us
  other arithmetic: 5.43 us -> 0 us
    all_gather x4 -> x0, waiting for transfers between devices: 136 us -> none  [the longest x1 41.4 us: body(): grads_all = lax.all_gather(gradient_rows, 'seq', axis=0, tiled=True)]
    pallas_call x0 -> x1, Pallas kernels: none -> 76.9 us  [fused_body(): pl.pallas_call(fused_kernel, out_shape=(jax.ShapeDtypeStruct((act, width)...]
    reduce_scatter x3 -> x0, waiting for transfers between devices: 63.8 us -> none  [the longest x1 30.8 us: body(): lax.psum_scatter(up_mid, 'dp', scatter_dimension=0, tiled=True)]
    all_gather x4 -> x0, blocking collectives: 39.9 us -> none  [the longest x1 12.8 us: body(): lax.all_gather(depths, 'seq', axis=0, tiled=True)]
    unnamed x9 -> x0, waiting for transfers between devices: 38 us -> none
    dot_general x9 -> x0, matrix products: 15.5 us -> none  [the longest x3 7.17 us: contract_final_axis(): lax.dot_general(left, right, (((1,), (1,)), ((), ())), preferred_element_...]
    gather x2 -> x0, local copies, waits for them, and re-layouts: 7.73 us -> none  [the longest x1 3.89 us: body(): picked = jnp.take(grads_all, jnp.maximum(packed_slot_index, 0), axis=0)]
    scatter x1 -> x0, local copies, waits for them, and re-layouts: 4.3 us -> none  [body(): source = jnp.zeros((act_rows,), jnp.int32).at[jnp.where(mine, pos_all, ac...]
  transfers between devices with their start and end apart: 8 -> 0, of which waited for: 8 -> 0; matrix products, arithmetic and copies ran while one was open for 8% -> 0% of each run, Pallas kernels for 0% -> 0%
where the time goes in v1:
time: 88.3 us; the launch traced here: 87.8 us
  Pallas kernels  76.9 us (87%)
  local copies, waits for them, and re-layouts  10.2 us (12%)
    pallas_call x1, Pallas kernels, fused_body(): pl.pallas_call(fused_kernel, out_shape=(jax.ShapeDtypeStruct((act, width)...  76.9 us
    unnamed x18, local copies, waits for them, and re-layouts  7.42 us

profile of v1, /device:TPU:0, one launch (start us, length us, event | category | flops | bytes accessed | tf_op | source)
XLA Modules:
  0.0 87.8 jit_solution(11870686727511375153)
XLA Ops:
  0.6 0.0 copy-start.5
  0.6 0.7 reshape.22.gain_b_ref
  1.3 0.0 copy-start.6
  1.4 0.7 reshape.23.gain_a_ref
  2.1 0.0 copy-done.5
  2.1 0.0 copy-done.6
  2.1 0.0 copy-start
  2.1 1.2 %copy-done = bf16[256,1792]{1,0:T(8,128)(2,1)S(1)} copy-done((bf16[256,1792]{1,0:T(8,128)(2,1)S(1)}, bf16[256,1792]{1,0:T(8,128)(2,1)}, u32[]{:S(2)}) %copy-start) | copy-done | bytes 917528
  3.3 0.0 copy-start.1
  3.3 1.0 %copy-done.1 = bf16[128,1792]{1,0:T(8,128)(2,1)S(1)} copy-done((bf16[128,1792]{1,0:T(8,128)(2,1)S(1)}, bf16[128,1792]{1,0:T(8,128)(2,1)}, u32[]{:S(2)}) %copy-start.1) | copy-done | bytes 458776
  4.3 0.0 copy-start.2
  4.3 1.0 %copy-done.2 = bf16[224,1024]{1,0:T(8,128)(2,1)S(1)} copy-done((bf16[224,1024]{1,0:T(8,128)(2,1)S(1)}, bf16[224,1024]{1,0:T(8,128)(2,1)}, u32[]{:S(2)}) %copy-start.2) | copy-done | bytes 458776
  5.3 0.0 copy-start.3
  5.3 1.0 %copy-done.3 = bf16[128,1792]{1,0:T(8,128)(2,1)S(1)} copy-done((bf16[128,1792]{1,0:T(8,128)(2,1)S(1)}, bf16[128,1792]{1,0:T(8,128)(2,1)}, u32[]{:S(2)}) %copy-start.3) | copy-done | bytes 458776
  6.3 0.0 copy-start.4
  6.3 0.8 copy-done.4
  7.1 0.0 copy-start.7
  7.1 0.7 copy-done.7
  7.8 76.9 %shard_map.129 = (bf16[128,1792]{1,0:T(8,128)(2,1)S(1)}, bf16[256,1792]{1,0:T(8,128)(2,1)S(1)}, f32[224,32]{1,0:T(8,128)S(1)}, f32[128,32]{1,0:T(8,128)S(1)}) custom-call(s32[1,256]{1,0:T(1,128)S(1)} %bitcast.2, s32[1,256]{1,0:T(1,128)S(1)} %bitcast.3, f32[1,1792]{1,0:T(1,128)S(1)} %reshape.22.gain_b_ref, f32[1,1792]{1,0:T(1,128)S(1)} %reshape.23.gain_a_ref, ...), custom_call_target="tpu_custom_call" | custom-call | tf_op jit(solution)/shard_map/pallas_call | solution.py:473
  84.7 0.7 copy.15
  85.4 0.7 copy.14
  86.1 0.8 copy.18
  86.9 0.9 %copy.19 = bf16[256,1792]{1,0:T(8,128)(2,1)} copy(bf16[256,1792]{1,0:T(8,128)(2,1)S(1)} %get-tuple-element.13) | data formatting | bytes 1835008
Async XLA Ops:
  0.6 1.4 %copy-start.5 = (bf16[128,128]{1,0:T(8,128)(2,1)S(1)}, bf16[128,128]{1,0:T(8,128)(2,1)}, u32[]{:S(2)}) copy-start(bf16[128,128]{1,0:T(8,128)(2,1)} %up_in.1) | copy-start | bytes 98308
  1.3 0.7 copy-start.6
  2.1 1.2 %copy-start = (bf16[256,1792]{1,0:T(8,128)(2,1)S(1)}, bf16[256,1792]{1,0:T(8,128)(2,1)}, u32[]{:S(2)}) copy-start(bf16[256,1792]{1,0:T(8,128)(2,1)} %hidden_hbm.1) | copy-start | bytes 2752516
  3.3 1.0 %copy-start.1 = (bf16[128,1792]{1,0:T(8,128)(2,1)S(1)}, bf16[128,1792]{1,0:T(8,128)(2,1)}, u32[]{:S(2)}) copy-start(bf16[128,1792]{1,0:T(8,128)(2,1)} %cot_hbm.1) | copy-start | bytes 1376260
  4.3 1.0 %copy-start.2 = (bf16[224,1024]{1,0:T(8,128)(2,1)S(1)}, bf16[224,1024]{1,0:T(8,128)(2,1)}, u32[]{:S(2)}) copy-start(bf16[224,1024]{1,0:T(8,128)(2,1)} %wv_in.1) | copy-start | bytes 1376260
  5.3 1.0 %copy-start.3 = (bf16[128,1792]{1,0:T(8,128)(2,1)S(1)}, bf16[128,1792]{1,0:T(8,128)(2,1)}, u32[]{:S(2)}) copy-start(bf16[128,1792]{1,0:T(8,128)(2,1)} %wo_in.1) | copy-start | bytes 1376260
  6.3 0.8 copy-start.4
  7.1 0.7 copy-start.7

commit v2 on v1

--- a/solution.py
+++ b/solution.py
@@ -154,7 +154,7 @@
 
 def fused_kernel(
     slot_ref, depth_ref, gain_b_ref, gain_a_ref, hidden_hbm, cot_hbm, wv_in, wo_in, dn_in, up_in,
-    looped_hbm, gh_hbm, down_out, up_out,
+    looped_hbm, gh_hbm, lora_out,
     wv, wo, dn, up, hid, cot, sendb, recvb, gsend, grecv, lsend, lrecv, zsend, zrecv,
     place, unplace, normed, low, proj, mixed, gv, gn, packed, looped,
     w_send, w_recv, s_send, s_recv, l_send, l_recv, g_send, g_recv, z_send, z_recv, loc,
@@ -166,6 +166,10 @@
     nbr_x, nbr_y, sib = dp + 2 - 4 * x, dp + 4 - 8 * y, dp + 1 - 2 * core
     diag = nbr_x + 4 - 8 * y
     to_sib = 1 - 2 * core
+    partner = seq + 1 - 2 * (seq % 2)
+    side = (core + seq) % 2
+    turn_from = nbr_x + side * (nbr_y - nbr_x)
+    turn_to = nbr_y + side * (nbr_x - nbr_y)
 
     local = [
         pltpu.make_async_copy(hidden_hbm, hid, loc.at[0]),
@@ -216,7 +220,7 @@
         part = rows // 2
         return full.at[pl.ds(pl.multiple_of(owner * rows + half * part, 16), part), :]
 
-    def piece(a, number, owner, half, target, from_input=False):
+    def piece(a, number, owner, half, target, from_input=False, at_seq=None):
         dst = region(a, owner, half)
         if from_input:
             shard = arrays[a][0]
@@ -226,7 +230,8 @@
             source = dst
         return pltpu.make_async_remote_copy(
             src_ref=source, dst_ref=dst, send_sem=w_send.at[a * 13 + number],
-            recv_sem=w_recv.at[a * 13 + number], device_id=(target, seq), device_id_type=MESH,
+            recv_sem=w_recv.at[a * 13 + number],
+            device_id=(target, seq if at_seq is None else at_seq), device_id_type=MESH,
         )
 
     pending = []
@@ -239,19 +244,20 @@
     def got(a, number, owner, half):
         piece(a, number, owner, half, sib).wait_recv()
 
-    def own(a):
+    def own_first(a):
         send(a, 0, dp, 0, nbr_x, from_input=True)
         send(a, 3, dp, 1, nbr_y, from_input=True)
+        send(a, 6, dp, None, sib, from_input=True)
+
+    def own_second(a):
         send(a, 1, dp, 1, nbr_x, from_input=True)
         send(a, 2, dp, 0, nbr_y, from_input=True)
-        send(a, 6, dp, None, sib, from_input=True)
 
     def forward_first(a):
         got(a, 0, nbr_x, 0)
-        send(a, 4, nbr_x, 0, nbr_y)
+        got(a, 3, nbr_y, 1)
+        send(a, 4, turn_from, side, turn_to)
         send(a, 7, nbr_x, 0, sib)
-        got(a, 3, nbr_y, 1)
-        send(a, 5, nbr_y, 1, nbr_x)
         send(a, 8, nbr_y, 1, sib)
 
     def forward_second(a):
@@ -261,10 +267,13 @@
         send(a, 10, nbr_y, 0, sib)
 
     def forward_diag(a):
-        got(a, 4, diag, 0)
-        send(a, 11, diag, 0, sib)
-        got(a, 5, diag, 1)
-        send(a, 12, diag, 1, sib)
+        got(a, 4, diag, side)
+        send(a, 5, diag, side, dp, at_seq=partner)
+        send(a, 11, diag, side, sib)
+
+    def forward_partner(a):
+        got(a, 5, diag, 1 - side)
+        send(a, 12, diag, 1 - side, sib)
 
     def finish(a):
         got(a, 6, sib, None)
@@ -272,11 +281,11 @@
         got(a, 8, nbr_y + to_sib, 1)
         got(a, 9, nbr_x + to_sib, 1)
         got(a, 10, nbr_y + to_sib, 0)
-        got(a, 11, diag + to_sib, 0)
-        got(a, 12, diag + to_sib, 1)
-
-    for a in (0, 1, 2):
-        own(a)
+        got(a, 11, diag + to_sib, 1 - side)
+        got(a, 12, diag + to_sib, side)
+
+    for a in (0, 1, 2, 3):
+        own_first(a)
 
     def block(owner, rows):
         return pl.ds(pl.multiple_of(owner * rows, 16), rows)
@@ -306,9 +315,17 @@
 
     for a in (0, 1, 2):
         forward_first(a)
-    own(3)
+    for a in (0, 1, 2):
+        own_second(a)
+    forward_first(3)
+    own_second(3)
+    for a in (0, 1, 2):
+        forward_diag(a)
     for a in (0, 1, 2):
         forward_second(a)
+    forward_diag(3)
+    for a in (0, 1, 2):
+        forward_partner(a)
 
     for k in (1, 2, 3):
         arrival(sendb, recvb, s_send, s_recv, k)
@@ -317,10 +334,8 @@
     x_float = dot(unplace[...], recvb[:, :width], 0, 0)
     packed[...] = x_float
     inv_pre = lax.rsqrt(jnp.mean(x_float * x_float, axis=-1, keepdims=True) + epsilon)
-    normed[...] = (x_float * inv_pre * gain_b_ref[...]).astype(BF)
-
-    for a in (0, 1, 2):
-        forward_diag(a)
+    normed[...] = (x_float * inv_pre * gain_b_ref[...].reshape(1, width)).astype(BF)
+
     for copy in local[1:]:
         copy.wait()
     for a in (0, 1, 2):
@@ -337,9 +352,8 @@
             dot(normed[...], wv[:, at]) + dot(low[...], up[at, :], 1, 1)
         ).astype(BF)
 
-    forward_first(3)
     forward_second(3)
-    forward_diag(3)
+    forward_partner(3)
     finish(3)
 
     @pl.loop(0, width // tile)
@@ -350,7 +364,7 @@
     m = mixed[...]
     inv_post = lax.rsqrt(jnp.mean(m * m, axis=-1, keepdims=True) + epsilon)
     shaped = m * inv_post
-    gain_a = gain_a_ref[...]
+    gain_a = gain_a_ref[...].reshape(1, width)
     looped[...] = (packed[...] + shaped * gain_a).astype(BF)
     loop_out = pltpu.make_async_copy(looped, looped_hbm, loc.at[6])
     loop_out.start()
@@ -366,7 +380,28 @@
 
     grad_low = dot(gv[...], up[...]).astype(BF)
 
-    down_rows, up_rows = down_out.shape[0], up_out.shape[0]
+    @pl.loop(0, width // tile)
+    def _(n):
+        at = pl.ds(pl.multiple_of(n * tile, tile), tile)
+        gn[:, at] = dot(gv[...], wv[at, :], 1, 1) + dot(grad_low, dn[at, :], 1, 1)
+
+    x_float = packed[...]
+    inv_pre = lax.rsqrt(jnp.mean(x_float * x_float, axis=-1, keepdims=True) + epsilon)
+    whitened = x_float * inv_pre
+    grad_white = gn[...] * gain_b_ref[...].reshape(1, width)
+    grad_packed = (
+        cot[...].astype(F32)
+        + inv_pre
+        * (grad_white - whitened * jnp.mean(grad_white * whitened, axis=-1, keepdims=True))
+    ).astype(BF)
+    gsend[...] = dot(unplace[...], grad_packed).astype(BF)
+    for k in (2, 1, 3):
+        copy = exchange(gsend, grecv, g_send, g_recv, k)
+        copy.start()
+        pending.append(copy)
+    grecv[block(seq, CAP), :] = gsend[block(seq, CAP), :]
+
+    down_rows, up_rows = dn_in.shape[0], up_in.shape[0]
     down_term = dot(normed[...], grad_low, 0, 0).astype(BF)
     up_term = dot(gv[...], low[...], 0, 0).astype(BF)
     for owner in range(n_dp):
@@ -382,27 +417,6 @@
         pending.append(copy)
     lrecv[dp] = lsend[dp]
 
-    @pl.loop(0, width // tile)
-    def _(n):
-        at = pl.ds(pl.multiple_of(n * tile, tile), tile)
-        gn[:, at] = dot(gv[...], wv[at, :], 1, 1) + dot(grad_low, dn[at, :], 1, 1)
-
-    x_float = packed[...]
-    inv_pre = lax.rsqrt(jnp.mean(x_float * x_float, axis=-1, keepdims=True) + epsilon)
-    whitened = x_float * inv_pre
-    grad_white = gn[...] * gain_b_ref[...]
-    grad_packed = (
-        cot[...].astype(F32)
-        + inv_pre
-        * (grad_white - whitened * jnp.mean(grad_white * whitened, axis=-1, keepdims=True))
-    ).astype(BF)
-    gsend[...] = dot(unplace[...], grad_packed).astype(BF)
-    for k in (2, 1, 3):
-        copy = exchange(gsend, grecv, g_send, g_recv, k)
-        copy.start()
-        pending.append(copy)
-    grecv[block(seq, CAP), :] = gsend[block(seq, CAP), :]
-
     for k in range(1, n_dp):
         origin = (dp + n_dp - k) % n_dp
         here = lrecv.at[origin]
@@ -416,18 +430,18 @@
     lead = total.shape[0]
     pad = zsend.shape[1] - lead
     total = jnp.concatenate([total, jnp.zeros((pad, total.shape[1]), F32)], axis=0)
-    zsend[...] = total.T
-    cols = down_out.shape[1]
+    zsend[...] = total.T.astype(BF)
+    cols = lora_out.shape[0]
     for k in range(1, n_seq):
         target = (seq + k) % n_seq
         copy = pltpu.make_async_remote_copy(
-            src_ref=zsend.at[pl.ds(pl.multiple_of(target * cols, 8), cols), :],
+            src_ref=zsend.at[pl.ds(pl.multiple_of(target * cols, 16), cols), :],
             dst_ref=zrecv.at[seq], send_sem=z_send.at[k], recv_sem=z_recv.at[k],
             device_id=(dp, target), device_id_type=MESH,
         )
         copy.start()
         pending.append(copy)
-    zrecv[seq] = zsend[pl.ds(pl.multiple_of(seq * cols, 8), cols), :]
+    zrecv[seq] = zsend[pl.ds(pl.multiple_of(seq * cols, 16), cols), :]
 
     for k in (1, 2, 3):
         arrival(gsend, grecv, g_send, g_recv, k)
@@ -443,10 +457,8 @@
             device_id=(dp, origin), device_id_type=MESH,
         ).wait_recv()
     grad_scale = 1.0 / math.sqrt(n_seq * cot.shape[0] * n_dp)
-    mine = ((zrecv[0] + zrecv[1]) + (zrecv[2] + zrecv[3])) * grad_scale
-    mine = jnp.concatenate([mine, jnp.zeros((128 - cols, mine.shape[1]), F32)], axis=0).T
-    down_out[...] = mine[:down_rows, :cols]
-    up_out[...] = mine[down_rows:lead, :cols]
+    z = [zrecv[owner].astype(F32) for owner in range(n_seq)]
+    lora_out[...] = ((z[0] + z[1]) + (z[2] + z[3])) * grad_scale
     for copy in pending:
         copy.wait_send()
     loop_out.wait()
@@ -467,19 +479,18 @@
     cols = rank // n_seq
     lead = v_rows + u_rows
     lead_pad = -(-lead // 128) * 128
-    vm, hbm = pl.BlockSpec(memory_space=pltpu.VMEM), pl.BlockSpec(memory_space=pl.ANY)
+    vm, hbm = pl.BlockSpec(memory_space=pltpu.VMEM), pl.BlockSpec(memory_space=pltpu.HBM)
     dma = pltpu.SemaphoreType.DMA
     rows = n_seq * CAP
-    return pl.pallas_call(
+    looped, grad_hidden, lora = pl.pallas_call(
         fused_kernel,
         out_shape=(
             jax.ShapeDtypeStruct((act, width), BF),
             jax.ShapeDtypeStruct((tok, width), BF),
-            jax.ShapeDtypeStruct((v_rows, cols), F32),
-            jax.ShapeDtypeStruct((u_rows, cols), F32),
+            jax.ShapeDtypeStruct((cols, lead_pad), F32),
         ),
         in_specs=[vm] * 4 + [hbm] * 6,
-        out_specs=(hbm, hbm, vm, vm),
+        out_specs=(hbm, hbm, vm),
         scratch_shapes=[
             pltpu.VMEM((v_rows * n_dp, value_width), BF),
             pltpu.VMEM((o_rows * n_dp, width), BF),
@@ -493,8 +504,8 @@
             pltpu.VMEM((rows, width), BF),
             pltpu.VMEM((n_dp, lead, rank), BF),
             pltpu.VMEM((n_dp, lead, rank), BF),
-            pltpu.VMEM((rank, lead_pad), F32),
-            pltpu.VMEM((n_seq, cols, lead_pad), F32),
+            pltpu.VMEM((rank, lead_pad), BF),
+            pltpu.VMEM((n_seq, cols, lead_pad), BF),
             pltpu.VMEM((rows, tok), BF),
             pltpu.VMEM((rows, 128), BF),
             pltpu.VMEM((act, width), BF),
@@ -509,13 +520,13 @@
             dma((4,)), dma((4,)), dma((4,)), dma((4,)), dma((8,)),
         ],
         compiler_params=pltpu.CompilerParams(
-            collective_id=0, has_side_effects=True, vmem_limit_bytes=48 << 20
+            collective_id=0, has_side_effects=True, vmem_limit_bytes=62 << 20
         ),
     )(
         packed_slot_index.reshape(1, tok),
         depths.reshape(1, tok),
-        before_norm_gain.reshape(1, width),
-        after_norm_gain.reshape(1, width),
+        before_norm_gain,
+        after_norm_gain,
         hidden,
         cotangent,
         value_weight,
@@ -523,6 +534,7 @@
         adapter_down_factor,
         adapter_up_factor,
     )
+    return looped, grad_hidden, lora[:, :v_rows].T, lora[:, v_rows:lead].T
 
 
 def body(*arrays):

time: 88.3 us -> 80.1 us (0.907)
  local copies, waits for them, and re-layouts: 10.2 us -> 5.63 us
  Pallas kernels: 76.9 us -> 73.5 us
    unnamed x18 -> x4, local copies, waits for them, and re-layouts: 7.42 us -> 2.74 us
    pallas_call x1, Pallas kernels: 76.9 us -> 73.5 us  [fused_body(): pl.pallas_call(fused_kernel, out_shape=(jax.ShapeDtypeStruct((act, width)...]
    transpose x0 -> x2, local copies, waits for them, and re-layouts: none -> 2.89 us  [fused_body(): return (looped, grad_hidden, lora[:, :v_rows].T, lora[:, v_rows:lead].T)]
    reshape x2 -> x0, local copies, waits for them, and re-layouts: 1.42 us -> none  [the longest x1 0.72 us: fused_body(): after_norm_gain.reshape(1, width)]
    pallas_call x2 -> x0, local copies, waits for them, and re-layouts: 1.37 us -> none  [fused_body(): pl.pallas_call(fused_kernel, out_shape=(jax.ShapeDtypeStruct((act, width)...]
where the time goes in v2:
time: 80.1 us; the launch traced here: 79.8 us
  Pallas kernels  73.5 us (92%)
  local copies, waits for them, and re-layouts  5.63 us (7%)
    pallas_call x1, Pallas kernels, fused_body(): pl.pallas_call(fused_kernel, out_shape=(jax.ShapeDtypeStruct((act, width)...  73.5 us
    transpose x2, local copies, waits for them, and re-layouts, fused_body(): return (looped, grad_hidden, lora[:, :v_rows].T, lora[:, v_rows:lead].T)  2.89 us
    unnamed x4, local copies, waits for them, and re-layouts  2.74 us

profile of v2, /device:TPU:0, one launch (start us, length us, event | category | flops | bytes accessed | tf_op | source)
XLA Modules:
  0.0 79.8 jit_solution(7026917651223762402)
XLA Ops:
  0.6 73.5 %shard_map.129 = (bf16[128,1792]{1,0:T(8,128)(2,1)}, bf16[256,1792]{1,0:T(8,128)(2,1)}, f32[32,384]{1,0:T(8,128)}) custom-call(s32[1,256]{1,0:T(1,128)} %bitcast.6, s32[1,256]{1,0:T(1,128)} %bitcast.7, f32[1792]{0:T(1024)} %gain_b_ref.1, f32[1792]{0:T(1024)} %gain_a_ref.1, bf16[256,1792]{1,0:T(8,128)(2,1)} %hidden_hbm.1, bf16[128,1792]{1,0:T(8,128)(2,1)} %cot_hbm.1, ...), custom_call_target="tpu_custom_call" | custom-call | tf_op jit(solution)/shard_map/pallas_call | solution.py:485
  74.2 0.0 copy-start
  74.2 1.5 %slice_bitcast_fusion.1 = f32[128,32]{0,1:T(8,128)} fusion(f32[32,384]{1,0:T(8,128)} %get-tuple-element.9), kind=kLoop, calls=%fused_computation.1 | loop fusion | bytes 32768 | tf_op jit(solution)/shard_map/transpose | solution.py:537
  75.7 1.4 %slice_bitcast_fusion = f32[224,32]{0,1:T(8,128)} fusion(f32[32,384]{1,0:T(8,128)} %get-tuple-element.9), kind=kLoop, calls=%fused_computation | loop fusion | bytes 57344 | tf_op jit(solution)/shard_map/transpose | solution.py:537
  77.1 1.8 %copy.16 = bf16[128,1792]{1,0:T(8,128)(2,1)} copy(bf16[128,1792]{1,0:T(8,128)(2,1)} %get-tuple-element.14) | data formatting | bytes 917504
  78.9 0.0 copy-done
  78.9 0.9 %copy.17 = bf16[256,1792]{1,0:T(8,128)(2,1)} copy(bf16[256,1792]{1,0:T(8,128)(2,1)S(1)} %copy-done) | data formatting | bytes 1835008
Async XLA Ops:
  74.2 4.7 %copy-start = (bf16[256,1792]{1,0:T(8,128)(2,1)S(1)}, bf16[256,1792]{1,0:T(8,128)(2,1)}, u32[]{:S(2)}) copy-start(bf16[256,1792]{1,0:T(8,128)(2,1)} %get-tuple-element.15) | copy-start | bytes 2752516

commit v3 on v2

--- a/solution.py
+++ b/solution.py
@@ -313,18 +313,16 @@
         pending.append(copy)
     recvb[block(seq, CAP), :] = sendb[block(seq, CAP), :]
 
-    for a in (0, 1, 2):
+    for a in (0, 1, 2, 3):
         forward_first(a)
     for a in (0, 1, 2):
         own_second(a)
-    forward_first(3)
-    own_second(3)
-    for a in (0, 1, 2):
+    for a in (0, 1, 2, 3):
         forward_diag(a)
     for a in (0, 1, 2):
         forward_second(a)
-    forward_diag(3)
-    for a in (0, 1, 2):
+    own_second(3)
+    for a in (0, 1, 2, 3):
         forward_partner(a)
 
     for k in (1, 2, 3):
@@ -353,7 +351,6 @@
         ).astype(BF)
 
     forward_second(3)
-    forward_partner(3)
     finish(3)
 
     @pl.loop(0, width // tile)

time: 80.1 us -> 78.4 us (0.979)
  Pallas kernels: 73.5 us -> 71.9 us
    pallas_call x1, Pallas kernels: 73.5 us -> 71.9 us  [fused_body(): pl.pallas_call(fused_kernel, out_shape=(jax.ShapeDtypeStruct((act, width)...]
where the time goes in v3:
time: 78.4 us; the launch traced here: 78.2 us
  Pallas kernels  71.9 us (92%)
  local copies, waits for them, and re-layouts  5.63 us (7%)
    pallas_call x1, Pallas kernels, fused_body(): pl.pallas_call(fused_kernel, out_shape=(jax.ShapeDtypeStruct((act, width)...  71.9 us
    transpose x2, local copies, waits for them, and re-layouts, fused_body(): return (looped, grad_hidden, lora[:, :v_rows].T, lora[:, v_rows:lead].T)  2.89 us
    unnamed x4, local copies, waits for them, and re-layouts  2.74 us

profile of v3, /device:TPU:0, one launch (start us, length us, event | category | flops | bytes accessed | tf_op | source)
XLA Modules:
  0.0 78.2 jit_solution(15773289327631415394)
XLA Ops:
  0.6 71.9 %shard_map.129 = (bf16[128,1792]{1,0:T(8,128)(2,1)}, bf16[256,1792]{1,0:T(8,128)(2,1)}, f32[32,384]{1,0:T(8,128)}) custom-call(s32[1,256]{1,0:T(1,128)} %bitcast.6, s32[1,256]{1,0:T(1,128)} %bitcast.7, f32[1792]{0:T(1024)} %gain_b_ref.1, f32[1792]{0:T(1024)} %gain_a_ref.1, bf16[256,1792]{1,0:T(8,128)(2,1)} %hidden_hbm.1, bf16[128,1792]{1,0:T(8,128)(2,1)} %cot_hbm.1, ...), custom_call_target="tpu_custom_call" | custom-call | tf_op jit(solution)/shard_map/pallas_call | solution.py:482
  72.5 0.0 copy-start
  72.5 1.5 %slice_bitcast_fusion.1 = f32[128,32]{0,1:T(8,128)} fusion(f32[32,384]{1,0:T(8,128)} %get-tuple-element.9), kind=kLoop, calls=%fused_computation.1 | loop fusion | bytes 32768 | tf_op jit(solution)/shard_map/transpose | solution.py:534
  74.0 1.4 %slice_bitcast_fusion = f32[224,32]{0,1:T(8,128)} fusion(f32[32,384]{1,0:T(8,128)} %get-tuple-element.9), kind=kLoop, calls=%fused_computation | loop fusion | bytes 57344 | tf_op jit(solution)/shard_map/transpose | solution.py:534
  75.4 1.8 %copy.16 = bf16[128,1792]{1,0:T(8,128)(2,1)} copy(bf16[128,1792]{1,0:T(8,128)(2,1)} %get-tuple-element.14) | data formatting | bytes 917504
  77.2 0.0 copy-done
  77.2 0.9 %copy.17 = bf16[256,1792]{1,0:T(8,128)(2,1)} copy(bf16[256,1792]{1,0:T(8,128)(2,1)S(1)} %copy-done) | data formatting | bytes 1835008
Async XLA Ops:
  72.5 4.7 %copy-start = (bf16[256,1792]{1,0:T(8,128)(2,1)S(1)}, bf16[256,1792]{1,0:T(8,128)(2,1)}, u32[]{:S(2)}) copy-start(bf16[256,1792]{1,0:T(8,128)(2,1)} %get-tuple-element.15) | copy-start | bytes 2752516

commit v4 on v3

--- a/solution.py
+++ b/solution.py
@@ -343,7 +343,7 @@
 
     tile = 256
 
-    @pl.loop(0, proj.shape[1] // tile)
+    @pl.loop(0, proj.shape[1] // tile, unroll=True)
     def _(n):
         at = pl.ds(pl.multiple_of(n * tile, tile), tile)
         proj[:, at] = (
@@ -353,7 +353,7 @@
     forward_second(3)
     finish(3)
 
-    @pl.loop(0, width // tile)
+    @pl.loop(0, width // tile, unroll=True)
     def _(n):
         at = pl.ds(pl.multiple_of(n * tile, tile), tile)
         mixed[:, at] = dot(proj[...], wo[:, at])
@@ -370,14 +370,14 @@
         grad_shaped - shaped * jnp.mean(grad_shaped * shaped, axis=-1, keepdims=True)
     )
 
-    @pl.loop(0, gv.shape[1] // tile)
+    @pl.loop(0, gv.shape[1] // tile, unroll=True)
     def _(n):
         at = pl.ds(pl.multiple_of(n * tile, tile), tile)
         gv[:, at] = dot(mixed[...].astype(BF), wo[at, :], 1, 1).astype(BF)
 
     grad_low = dot(gv[...], up[...]).astype(BF)
 
-    @pl.loop(0, width // tile)
+    @pl.loop(0, width // tile, unroll=True)
     def _(n):
         at = pl.ds(pl.multiple_of(n * tile, tile), tile)
         gn[:, at] = dot(gv[...], wv[at, :], 1, 1) + dot(grad_low, dn[at, :], 1, 1)
@@ -517,7 +517,7 @@
             dma((4,)), dma((4,)), dma((4,)), dma((4,)), dma((8,)),
         ],
         compiler_params=pltpu.CompilerParams(
-            collective_id=0, has_side_effects=True, vmem_limit_bytes=62 << 20
+            collective_id=0, has_side_effects=True, vmem_limit_bytes=(64 << 20) - (400 << 10)
         ),
     )(
         packed_slot_index.reshape(1, tok),

time: 78.4 us -> 76.1 us (0.971)
  Pallas kernels: 71.9 us -> 69.5 us
    pallas_call x1, Pallas kernels: 71.9 us -> 69.5 us  [fused_body(): pl.pallas_call(fused_kernel, out_shape=(jax.ShapeDtypeStruct((act, width)...]
where the time goes in v4:
time: 76.1 us; the launch traced here: 75.8 us
  Pallas kernels  69.5 us (91%)
  local copies, waits for them, and re-layouts  5.63 us (7%)
    pallas_call x1, Pallas kernels, fused_body(): pl.pallas_call(fused_kernel, out_shape=(jax.ShapeDtypeStruct((act, width)...  69.5 us
    transpose x2, local copies, waits for them, and re-layouts, fused_body(): return (looped, grad_hidden, lora[:, :v_rows].T, lora[:, v_rows:lead].T)  2.89 us
    unnamed x4, local copies, waits for them, and re-layouts  2.74 us

profile of v4, /device:TPU:0, one launch (start us, length us, event | category | flops | bytes accessed | tf_op | source)
XLA Modules:
  0.0 75.8 jit_solution(9092632423764942987)
XLA Ops:
  0.6 69.5 %shard_map.129 = (bf16[128,1792]{1,0:T(8,128)(2,1)}, bf16[256,1792]{1,0:T(8,128)(2,1)}, f32[32,384]{1,0:T(8,128)}) custom-call(s32[1,256]{1,0:T(1,128)} %bitcast.6, s32[1,256]{1,0:T(1,128)} %bitcast.7, f32[1792]{0:T(1024)} %gain_b_ref.1, f32[1792]{0:T(1024)} %gain_a_ref.1, bf16[256,1792]{1,0:T(8,128)(2,1)} %hidden_hbm.1, bf16[128,1792]{1,0:T(8,128)(2,1)} %cot_hbm.1, ...), custom_call_target="tpu_custom_call" | custom-call | tf_op jit(solution)/shard_map/pallas_call | solution.py:482
  70.2 0.0 copy-start
  70.2 1.5 %slice_bitcast_fusion.1 = f32[128,32]{0,1:T(8,128)} fusion(f32[32,384]{1,0:T(8,128)} %get-tuple-element.9), kind=kLoop, calls=%fused_computation.1 | loop fusion | bytes 32768 | tf_op jit(solution)/shard_map/transpose | solution.py:534
  71.7 1.4 %slice_bitcast_fusion = f32[224,32]{0,1:T(8,128)} fusion(f32[32,384]{1,0:T(8,128)} %get-tuple-element.9), kind=kLoop, calls=%fused_computation | loop fusion | bytes 57344 | tf_op jit(solution)/shard_map/transpose | solution.py:534
  73.1 1.8 %copy.16 = bf16[128,1792]{1,0:T(8,128)(2,1)} copy(bf16[128,1792]{1,0:T(8,128)(2,1)} %get-tuple-element.14) | data formatting | bytes 917504
  74.9 0.0 copy-done
  74.9 0.9 %copy.17 = bf16[256,1792]{1,0:T(8,128)(2,1)} copy(bf16[256,1792]{1,0:T(8,128)(2,1)S(1)} %copy-done) | data formatting | bytes 1835008
Async XLA Ops:
  70.2 4.7 %copy-start = (bf16[256,1792]{1,0:T(8,128)(2,1)S(1)}, bf16[256,1792]{1,0:T(8,128)(2,1)}, u32[]{:S(2)}) copy-start(bf16[256,1792]{1,0:T(8,128)(2,1)} %get-tuple-element.15) | copy-start | bytes 2752516
